TPU v7x, 256 devices: a whole 4x4x8 slice. The times are simulated.
256 devices in a mesh: sess: 32 (over y_hi, z, core), dp: 4 (over x), fsdp: 2 (over y_lo).
Axes of the slice: x: 4, y: 4 (y_hi: 2, y_lo: 2; y = y_hi * 2 + y_lo), z: 8, core: 2. Of those that a mesh axis runs over, the one named last changes fastest.
Arguments:
- unit_tokens: bfloat16 [4096, 128, 1024], P(('sess', 'dp', 'fsdp')), may hold values from -6 to 6
- block_owner: int32 [4096, 1], P(('sess', 'dp', 'fsdp')), may hold values from 0 to 31; in each aligned block of 16 rows (0 to 15, 16 to 31, ...) at most 2 rows name the same one
- block_clip: int32 [4096], P(('sess', 'dp', 'fsdp')), may hold values from 0 to 1
- block_valid: int32 [4096], P(('sess', 'dp', 'fsdp')), may hold values from 1 to 128, as said below
- latent_query_rows: bfloat16 [32, 1024], replicated, may hold values from -600 to 600
- latents: bfloat16 [32, 1024], replicated, may hold values from -1.5 to 1.5
- w_kv: bfloat16 [1024, 512], P('fsdp'), may hold values from -0.1875 to 0.1875
- w_out: bfloat16 [1024, 1024], P('fsdp'), may hold values from -0.75 to 0.75
- w_proj: bfloat16 [1024, 512], P('fsdp'), may hold values from -0.1875 to 0.1875
- movie_frame_embeddings: bfloat16 [512, 512], replicated, may hold values from -6 to 6
- clip_frame: int32 [512], P(('sess', 'dp', 'fsdp')), may hold values from 0 to 511
- logit_scale: float32 [1], replicated, may hold values from 40 to 60
Outputs:
- latent_state: bfloat16 [512, 32, 1024], P(('sess', 'dp', 'fsdp'))
- clip_loss: float32 [512], P(('sess', 'dp', 'fsdp'))
Inputs may be any that keep to these rules, and one draw needn't show every extreme that they name: `block_owner`: among the 16 blocks of one device no index is named more than 2 times, a bound that some block reaches. `block_valid`: the first block of every device is full.
All inputs are finite; a program needn't handle non-finite values.
Results may differ from a plain program's by a relative error of at most 0.009.
The roundings to bfloat16 on the way count: a program that leaves them out, or rounds other values in their place, can miss the bound.
Values may be sent and summed in bfloat16 or wider, within the bound.
A program may use at most 128 MiB of HBM per device.

v0:
```python
import math
import jax
import jax.numpy as jnp
from jax import lax
from jax.sharding import PartitionSpec as P

HEADS = 16
HEAD_DIM = 64
KV_HEADS = 4


def fold_rows(left, piece):
    return jnp.dot(left, piece, preferred_element_type=jnp.float32)


def keys_folded(left, weight):
    return fold_rows(left, lax.all_gather(weight, "fsdp", axis=0, tiled=True))


def output_folded(left, weight):
    return fold_rows(left, lax.all_gather(weight, "fsdp", axis=0, tiled=True))


def embed_folded(left, weight):
    return fold_rows(left, lax.all_gather(weight, "fsdp", axis=0, tiled=True))


def per_device(
    unit_tokens,
    block_owner,
    block_clip,
    block_valid,
    latent_query_rows,
    latents,
    w_kv,
    w_out,
    w_proj,
    movie_frame_embeddings,
    clip_frame,
    logit_scale,
):
    peers = lax.axis_size("sess")
    blocks_here, block_rows, width = unit_tokens.shape
    capacity = max(2, (2 * blocks_here + peers - 1) // peers)
    slots_all = peers * capacity
    kv_width = w_kv.shape[1] // 2
    group_size = HEADS // KV_HEADS
    clips_here = clip_frame.shape[0]
    lat_rows = latent_query_rows.shape[0]
    scaling = 1.0 / math.sqrt(HEAD_DIM)
    target = block_owner[:, 0]
    peer_hits = (target[:, None] == jnp.arange(peers, dtype=jnp.int32)[None, :]).astype(jnp.int32)
    preceding_value = jnp.cumsum(peer_hits, axis=0) - peer_hits
    rank_within = jnp.sum(preceding_value * peer_hits, axis=1)
    slot_of = target * capacity + rank_within
    placing = (slot_of[:, None] == jnp.arange(slots_all, dtype=jnp.int32)[None, :]).astype(
        jnp.bfloat16
    )
    meta_rows = jnp.stack([block_valid, block_clip], axis=1).astype(jnp.bfloat16)
    slot_meta = jnp.einsum("bs,bx->sx", placing, meta_rows, preferred_element_type=jnp.bfloat16)
    slot_meta = slot_meta.reshape(peers, capacity, 2)
    packed = jnp.einsum(
        "bs,bx->sx",
        placing,
        unit_tokens.reshape(blocks_here, block_rows * width),
        preferred_element_type=jnp.bfloat16,
    )
    packed = packed.reshape(peers, capacity, block_rows * width)
    arrived, arrived_meta = (
        lax.all_to_all(packed, "sess", split_axis=0, concat_axis=0, tiled=True),
        lax.all_to_all(slot_meta, "sess", split_axis=0, concat_axis=0, tiled=True),
    )
    kv_slots = keys_folded(arrived.reshape(slots_all * block_rows, width), w_kv).astype(
        jnp.bfloat16
    )
    kv_slots = kv_slots.reshape(slots_all, block_rows, 2 * kv_width)
    meta_float = arrived_meta.astype(jnp.float32).reshape(slots_all, 2)
    valid_count = meta_float[:, 0]
    slot_clip = meta_float[:, 1].astype(jnp.int32)
    row_live = jnp.arange(block_rows).astype(jnp.float32)[None, :] < valid_count[:, None]
    member = (slot_clip[None, :] == jnp.arange(clips_here, dtype=jnp.int32)[:, None]) & (
        valid_count[None, :] > 0.0
    )
    member_float = member.astype(jnp.float32)
    keys = kv_slots[:, :, :kv_width].reshape(slots_all, block_rows, KV_HEADS, HEAD_DIM)
    value_rows = kv_slots[:, :, kv_width:].reshape(slots_all, block_rows, KV_HEADS, HEAD_DIM)
    query = latent_query_rows.reshape(lat_rows, HEADS, HEAD_DIM)
    head_parts = []
    for head_position in range(HEADS):
        key_value_head = head_position // group_size
        scores = (
            jnp.einsum(
                "wa,pha->wph",
                query[:, head_position],
                keys[:, :, key_value_head],
                preferred_element_type=jnp.float32,
            )
            * scaling
        )
        scores = jnp.where(row_live[None], scores, -jnp.inf)
        slot_top = jnp.max(scores, axis=-1)
        clip_top = jnp.max(jnp.where(member[:, None, :], slot_top[None, :, :], -jnp.inf), axis=-1)
        clip_top = jnp.maximum(clip_top, 0.0)
        slot_shift = jnp.take(clip_top, slot_clip, axis=0)
        soft_terms = jnp.exp(scores - jnp.transpose(slot_shift)[..., None])
        slot_total = jnp.sum(soft_terms, axis=-1)
        clip_total = jnp.sum(slot_total[None, :, :] * member_float[:, None, :], axis=-1) + jnp.exp(
            -clip_top
        )
        rounded_result = soft_terms.astype(jnp.bfloat16)
        slot_sums = jnp.einsum(
            "ori,rin->orn",
            rounded_result,
            value_rows[:, :, key_value_head],
            preferred_element_type=jnp.float32,
        )
        clip_sums = jnp.einsum(
            "lsd,cs->cld", slot_sums, member_float, precision=lax.Precision.HIGHEST
        )
        head_parts.append(clip_sums / clip_total[..., None])
    attention = jnp.concatenate(head_parts, axis=-1).astype(jnp.bfloat16)
    mixed = output_folded(attention.reshape(clips_here * lat_rows, width), w_out)
    state = latents.astype(jnp.float32)[None] + mixed.reshape(clips_here, lat_rows, width)
    latent_state = state.astype(jnp.bfloat16)
    pooled = jnp.mean(state, axis=1).astype(jnp.bfloat16)
    embed = embed_folded(pooled, w_proj)
    embed_unit = (embed / jnp.sqrt(jnp.sum(embed * embed, axis=-1, keepdims=True) + 1e-06)).astype(
        jnp.bfloat16
    )
    frames = jnp.take(movie_frame_embeddings, clip_frame, axis=0).astype(jnp.float32)
    frame_unit = (
        frames / jnp.sqrt(jnp.sum(frames * frames, axis=-1, keepdims=True) + 1e-06)
    ).astype(jnp.bfloat16)
    scale_value = logit_scale[0]
    own_pair = scale_value * jnp.sum(
        embed_unit.astype(jnp.float32) * frame_unit.astype(jnp.float32), axis=-1
    )
    smallest_value = jnp.full((clips_here,), -jnp.inf, jnp.float32)
    nothing = jnp.zeros((clips_here,), jnp.float32)
    row_top = smallest_value
    row_sum = nothing
    col_top = smallest_value
    col_sum = nothing
    other_embed = lax.all_gather(embed_unit, ("sess", "dp", "fsdp"), axis=0, tiled=True)
    other_frame = lax.all_gather(frame_unit, ("sess", "dp", "fsdp"), axis=0, tiled=True)
    row_logit = scale_value * jnp.dot(embed_unit, other_frame.T, preferred_element_type=jnp.float32)
    col_logit = scale_value * jnp.dot(frame_unit, other_embed.T, preferred_element_type=jnp.float32)
    row_next = jnp.max(row_logit, axis=1)
    col_next = jnp.max(col_logit, axis=1)
    row_sum = row_sum * jnp.exp(row_top - row_next) + jnp.sum(
        jnp.exp(row_logit - row_next[:, None]), axis=1
    )
    col_sum = col_sum * jnp.exp(col_top - col_next) + jnp.sum(
        jnp.exp(col_logit - col_next[:, None]), axis=1
    )
    row_top, row_sum, col_top, col_sum = (row_next, row_sum, col_next, col_sum)
    clip_loss = 0.5 * (row_top + jnp.log(row_sum) + col_top + jnp.log(col_sum)) - own_pair
    return (latent_state, clip_loss)


def solution(mesh):
    return jax.shard_map(
        per_device,
        mesh=mesh,
        in_specs=(
            P(("sess", "dp", "fsdp"), None, None),
            P(("sess", "dp", "fsdp"), None),
            P(("sess", "dp", "fsdp")),
            P(("sess", "dp", "fsdp")),
            P(),
            P(),
            P("fsdp", None),
            P("fsdp", None),
            P("fsdp", None),
            P(),
            P(("sess", "dp", "fsdp")),
            P(),
        ),
        out_specs=(P(("sess", "dp", "fsdp"), None, None), P(("sess", "dp", "fsdp"))),
        check_vma=False,
    )
```

profile of v0, /device:TPU:8, one launch (start us, length us, event | category | flops | bytes accessed | tf_op | source)
XLA Modules:
  0.0 1890.5 jit_solution(8112834568392189841)
XLA Ops:
  11.1 10.6 all-to-all-start
  21.7 4.8 reshape.604
  26.5 7.1 fusion.134
  33.6 31.8 %copy.220 = bf16[32,2,131072]{2,1,0:T(2,128)(2,1)} copy(bf16[32,2,131072]{2,0,1:T(8,128)(2,1)S(1)} %fusion.134) | data formatting | bytes 33554432 | tf_op jit(solution)/shard_map/bs,bx->sx/dot_general | solution.py:62
  65.4 10.1 all-to-all-start.1
  80.1 366.0 %all-to-all-done.1 = bf16[32,2,131072]{2,1,0:T(2,128)(2,1)} async-done(((bf16[32,2,131072]{2,1,0:T(2,128)(2,1)}), bf16[32,2,131072]{2,1,0:T(2,128)(2,1)}, u32[]{:S(2)}, u32[]{:S(2)}) %all-to-all-start.1) | async-done | bytes 16777248 | tf_op jit(solution)/shard_map/all_to_all | solution.py:70
  446.1 29.1 %reshape.408 = bf16[8192,1024]{1,0:T(8,128)(2,1)} reshape(bf16[32,2,131072]{2,1,0:T(2,128)(2,1)} %all-to-all-done.1) | data formatting | bytes 33554432 | tf_op jit(solution)/shard_map/reshape | solution.py:73
  475.3 12.7 convolution_convert_fusion
  488.0 3.6 fusion.167
  491.6 6.6 copy.310
  498.2 1.7 fusion.185
  500.0 1.7 fusion.171
  501.8 2.7 fusion.172
  504.5 2.6 fusion.173
  507.2 2.6 fusion.174
  509.8 2.6 fusion.175
  512.4 2.6 fusion.176
  515.1 2.6 fusion.177
  517.8 2.6 fusion.178
  520.4 2.6 fusion.179
  523.1 2.6 fusion.180
  525.7 2.6 fusion.181
  528.4 2.6 fusion.182
  531.0 2.6 fusion.183
  533.7 2.6 fusion.184
  536.3 2.6 fusion.170
  548.9 6.8 copy.308
  555.9 2.0 fusion.99
  557.9 3.3 convolution_bitcast_fusion
  561.8 1.7 convolution_bitcast_fusion.1
  564.2 1.7 convolution_bitcast_fusion.2
  566.6 1.7 convolution_bitcast_fusion.3
  568.9 1.7 convolution_bitcast_fusion.4
  571.3 1.7 convolution_bitcast_fusion.5
  573.7 1.8 convolution_bitcast_fusion.6
  576.1 1.7 convolution_bitcast_fusion.7
  578.5 1.7 convolution_bitcast_fusion.8
  580.8 1.9 convolution_bitcast_fusion.9
  583.4 1.7 convolution_bitcast_fusion.10
  585.8 1.7 convolution_bitcast_fusion.11
  588.1 1.7 convolution_bitcast_fusion.12
  590.5 1.7 convolution_bitcast_fusion.13
  592.8 1.8 convolution_bitcast_fusion.14
  598.4 2.3 fusion.52
  600.7 2.3 fusion.51
  603.0 1.0 fusion.50
  604.1 2.3 fusion.49
  606.4 2.5 fusion.48
  608.9 2.3 fusion.47
  611.2 2.3 fusion.46
  613.5 2.2 fusion.45
  615.8 1.0 fusion.44
  616.8 1.0 fusion.43
  617.9 1.0 fusion.42
  618.9 1.0 fusion.41
  620.0 1.0 fusion.40
  621.0 1.0 fusion.39
  622.1 1.0 fusion.38
  623.1 2.0 convolution_bitcast_fusion.15
  625.1 1.3 fusion.37
  627.2 2.7 fusion.168
  629.9 1.6 multiply_reduce_fusion.17
  631.7 623.4 %all-gather = bf16[256,2,512]{2,1,0:T(2,128)(2,1)S(1)} all-gather(bf16[1,2,512]{2,1,0:T(2,128)(2,1)S(1)} %bitcast.394), channel_id=1, replica_groups=mesh['sess'=32,'dp'=4,'fsdp'=2] {'sess','dp','fsdp'}, dimensions={0}, use_global_device_ids=true | all-gather | bytes 526336 | tf_op jit(solution)/shard_map/all_gather | solution.py:145
  1255.3 626.3 %all-gather.1 = bf16[256,2,512]{2,1,0:T(2,128)(2,1)S(1)} all-gather(bf16[1,2,512]{2,1,0:T(2,128)(2,1)S(1)} %bitcast.395), channel_id=1, replica_groups=mesh['sess'=32,'dp'=4,'fsdp'=2] {'sess','dp','fsdp'}, dimensions={0}, use_global_device_ids=true | all-gather | bytes 526336 | tf_op jit(solution)/shard_map/all_gather | solution.py:144
  (215 shorter events, 34.5 us)
Async XLA Ops:
  7.2 71.5 %copy-start = (bf16[512,512]{1,0:T(8,128)(2,1)S(1)}, bf16[512,512]{1,0:T(8,128)(2,1)}, u32[]{:S(2)}) copy-start(bf16[512,512]{1,0:T(8,128)(2,1)} %param.23) | copy-start | bytes 1572868
  11.1 54.3 %all-to-all-start = ((bf16[32,2,2]{1,2,0:T(2,128)(2,1)}), bf16[32,2,2]{1,2,0:T(2,128)(2,1)S(1)}, u32[]{:S(2)}, u32[]{:S(2)}) async-start(bf16[32,2,2]{1,2,0:T(2,128)(2,1)} %copy.217), calls=%async_computation | async-start | bytes 32768 | tf_op jit(solution)/shard_map/all_to_all | solution.py:71
  65.4 12.3 copy-start.24
  65.4 12.5 copy-start.25
  65.4 13.2 copy-start.26
  65.4 380.7 %all-to-all-start.1 = ((bf16[32,2,131072]{2,1,0:T(2,128)(2,1)}), bf16[32,2,131072]{2,1,0:T(2,128)(2,1)}, u32[]{:S(2)}, u32[]{:S(2)}) async-start(bf16[32,2,131072]{2,1,0:T(2,128)(2,1)} %copy.220), calls=%async_computation.1 | async-start | bytes 33554432 | tf_op jit(solution)/shard_map/all_to_all | solution.py:70
  75.5 399.7 %all-gather.6.cloned.1.call-start = ((), (), s32[]{:S(2)}) async-start(), calls=%async_computation.2 | async-start | bytes 1572864 | tf_op jit(solution)/shard_map/all_gather | solution.py:17
  76.3 550.9 %all-gather.8.cloned.1.call-start = ((), (), s32[]{:S(2)}) async-start(), calls=%async_computation.3 | async-start | bytes 3145728 | tf_op jit(solution)/shard_map/all_gather | solution.py:21
  77.0 552.9 %all-gather.10.cloned.1.call-start = ((), (), s32[]{:S(2)}) async-start(), calls=%async_computation.4 | async-start | bytes 1572864 | tf_op jit(solution)/shard_map/all_gather | solution.py:25
  555.7 5.4 copy-start.15
  555.7 6.1 copy-start.2
  555.9 7.7 copy-start.14
  561.1 4.8 copy-start.13
  563.5 4.7 copy-start.12
  565.9 4.7 copy-start.11
  568.3 4.8 copy-start.10
  570.7 4.8 copy-start.9
  573.0 4.8 copy-start.8
  575.5 4.7 copy-start.7
  577.8 5.0 copy-start.6
  580.2 5.0 copy-start.5
  582.8 4.7 copy-start.4
  585.1 4.7 copy-start.3
  594.6 8.4 copy-start.16
  598.4 17.4 copy-start.17
  600.7 16.1 copy-start.18
  603.0 14.8 copy-start.19
  604.1 14.8 copy-start.20
  606.4 13.6 copy-start.21
  608.9 12.1 copy-start.22
  611.2 10.9 copy-start.23
  625.1 1258.4 %copy-start.1 = (bf16[512,512]{1,0:T(8,128)(2,1)S(1)}, bf16[512,512]{1,0:T(8,128)(2,1)}, u32[]{:S(2)}) copy-start(bf16[512,512]{1,0:T(8,128)(2,1)} %param.23) | copy-start | bytes 1572868
Sparse Core Ops, SparseCore 0:
  78.1 54.6 all-gather.5
  134.6 56.9 all-gather.7
  193.4 53.8 all-gather.9
where the time goes:
time: 1900 us; the launch traced here: 1890 us
  blocking collectives  1250 us (66%)
  waiting for transfers between devices  368 us (19%)
  matrix products  120 us (6%)
  local copies, waits for them, and re-layouts  99.2 us (5%)
  starting transfers between devices  20.8 us (1%)
    all_gather x1, blocking collectives, per_device(): lax.all_gather(embed_unit, ('sess', 'dp', 'fsdp'), axis=0, tiled=True)  626 us
    all_gather x1, blocking collectives, per_device(): lax.all_gather(frame_unit, ('sess', 'dp', 'fsdp'), axis=0, tiled=True)  623 us
    all_to_all x1, waiting for transfers between devices, per_device(): lax.all_to_all(packed, 'sess', split_axis=0, concat_axis=0, tiled=True)  366 us
    dot_general x16, matrix products, per_device(): jnp.einsum('wa,pha->wph', query[:, head_position], keys[:, :, key_value_h...  39.7 us
  transfers between devices with their start and end apart: 5, of which 1 were waited for; matrix products, arithmetic and copies ran while one was open for 12% of the time, Pallas kernels for 0%

commit v1 on v0

--- a/solution.py
+++ b/solution.py
@@ -142,7 +142,15 @@
     col_top = smallest_value
     col_sum = nothing
     other_embed = lax.all_gather(embed_unit, ("sess", "dp", "fsdp"), axis=0, tiled=True)
-    other_frame = lax.all_gather(frame_unit, ("sess", "dp", "fsdp"), axis=0, tiled=True)
+    other_frame = jnp.concatenate(
+        lax.all_to_all(
+            jnp.stack([frame_unit] * lax.axis_size(("sess", "dp", "fsdp"))),
+            ("sess", "dp", "fsdp"),
+            0,
+            0,
+        ),
+        axis=0,
+    )
     row_logit = scale_value * jnp.dot(embed_unit, other_frame.T, preferred_element_type=jnp.float32)
     col_logit = scale_value * jnp.dot(frame_unit, other_embed.T, preferred_element_type=jnp.float32)
     row_next = jnp.max(row_logit, axis=1)

time: 1900 us -> 1300 us (0.68)
  blocking collectives: 1250 us -> 630 us
    all_gather x1 -> x0, blocking collectives: 623 us -> none  [per_device(): lax.all_gather(frame_unit, ('sess', 'dp', 'fsdp'), axis=0, tiled=True)]
  transfers between devices with their start and end apart: 5 -> 6, of which waited for: 1 -> 1; matrix products, arithmetic and copies ran while one was open for 12% -> 18% of each run, Pallas kernels for 0% -> 0%
where the time goes in v1:
time: 1300 us; the launch traced here: 1290 us
  blocking collectives  630 us (48%)
  waiting for transfers between devices  369 us (28%)
  matrix products  120 us (9%)
  local copies, waits for them, and re-layouts  100 us (8%)
  starting transfers between devices  34.1 us (3%)
  other arithmetic  16.8 us (1%)
  between operations  15.7 us (1%)
    all_gather x1, blocking collectives, per_device(): lax.all_gather(embed_unit, ('sess', 'dp', 'fsdp'), axis=0, tiled=True)  630 us
    all_to_all x1, waiting for transfers between devices, per_device(): lax.all_to_all(packed, 'sess', split_axis=0, concat_axis=0, tiled=True)  367 us
    dot_general x16, matrix products, per_device(): jnp.einsum('wa,pha->wph', query[:, head_position], keys[:, :, key_value_h...  39.7 us
    dot_general x1, local copies, waits for them, and re-layouts, per_device(): jnp.einsum('bs,bx->sx', placing, unit_tokens.reshape(blocks_here, block_r...  31.8 us
    dot_general x16, matrix products, per_device(): jnp.einsum('ori,rin->orn', rounded_result, value_rows[:, :, key_value_hea...  29.6 us
    reshape x1, local copies, waits for them, and re-layouts, per_device(): arrived.reshape(slots_all * block_rows, width)  29.1 us
  transfers between devices with their start and end apart: 6, of which 1 were waited for; matrix products, arithmetic and copies ran while one was open for 18% of the time, Pallas kernels for 0%

profile of v1, /device:TPU:8, one launch (start us, length us, event | category | flops | bytes accessed | tf_op | source)
XLA Modules:
  0.0 1285.9 jit_solution(863729279433101412)
XLA Ops:
  11.1 10.6 all-to-all-start
  21.7 4.8 reshape.620
  26.5 7.1 fusion.134
  33.6 31.8 %copy.220 = bf16[32,2,131072]{2,1,0:T(2,128)(2,1)} copy(bf16[32,2,131072]{2,0,1:T(8,128)(2,1)S(1)} %fusion.134) | data formatting | bytes 33554432 | tf_op jit(solution)/shard_map/bs,bx->sx/dot_general | solution.py:62
  65.4 10.1 all-to-all-start.1
  79.5 366.7 %all-to-all-done.1 = bf16[32,2,131072]{2,1,0:T(2,128)(2,1)} async-done(((bf16[32,2,131072]{2,1,0:T(2,128)(2,1)}), bf16[32,2,131072]{2,1,0:T(2,128)(2,1)}, u32[]{:S(2)}, u32[]{:S(2)}) %all-to-all-start.1) | async-done | bytes 16777248 | tf_op jit(solution)/shard_map/all_to_all | solution.py:70
  446.1 29.1 %reshape.425 = bf16[8192,1024]{1,0:T(8,128)(2,1)} reshape(bf16[32,2,131072]{2,1,0:T(2,128)(2,1)} %all-to-all-done.1) | data formatting | bytes 33554432 | tf_op jit(solution)/shard_map/reshape | solution.py:73
  475.3 12.7 convolution_convert_fusion
  488.0 3.6 fusion.167
  491.6 6.6 copy.310
  498.2 1.7 fusion.185
  500.0 1.7 fusion.171
  501.8 2.7 fusion.172
  504.5 2.6 fusion.173
  507.2 2.6 fusion.174
  509.8 2.6 fusion.175
  512.4 2.6 fusion.176
  515.1 2.6 fusion.177
  517.8 2.6 fusion.178
  520.4 2.6 fusion.179
  523.1 2.6 fusion.180
  525.7 2.6 fusion.181
  528.4 2.6 fusion.182
  531.0 2.6 fusion.183
  533.7 2.6 fusion.184
  536.3 2.6 fusion.170
  548.9 6.8 copy.308
  555.9 2.0 fusion.99
  557.9 3.3 convolution_bitcast_fusion
  561.8 1.7 convolution_bitcast_fusion.1
  564.2 1.7 convolution_bitcast_fusion.2
  566.6 1.7 convolution_bitcast_fusion.3
  568.9 1.7 convolution_bitcast_fusion.4
  571.3 1.7 convolution_bitcast_fusion.5
  573.7 1.8 convolution_bitcast_fusion.6
  576.1 1.7 convolution_bitcast_fusion.7
  578.5 1.7 convolution_bitcast_fusion.8
  580.8 1.9 convolution_bitcast_fusion.9
  583.4 1.7 convolution_bitcast_fusion.10
  585.8 1.7 convolution_bitcast_fusion.11
  588.1 1.7 convolution_bitcast_fusion.12
  590.5 1.7 convolution_bitcast_fusion.13
  592.8 1.8 convolution_bitcast_fusion.14
  598.4 2.3 fusion.52
  600.7 2.3 fusion.51
  603.0 1.0 fusion.50
  604.1 2.3 fusion.49
  606.4 2.5 fusion.48
  608.9 2.3 fusion.47
  611.2 2.3 fusion.46
  613.5 2.2 fusion.45
  615.8 1.0 fusion.44
  616.8 1.0 fusion.43
  617.9 1.0 fusion.42
  618.9 1.0 fusion.41
  620.0 1.0 fusion.40
  621.0 1.0 fusion.39
  623.1 2.0 convolution_bitcast_fusion.15
  625.1 1.3 fusion.37
  627.2 2.7 fusion.168
  629.9 1.6 multiply_reduce_fusion.17
  631.7 1.1 stack.14
  632.8 13.3 %all-to-all-start.2 = ((bf16[256,2,512]{2,1,0:T(2,128)(2,1)}), bf16[256,2,512]{2,1,0:T(2,128)(2,1)S(1)}, u32[]{:S(2)}, u32[]{:S(2)}) async-start(bf16[256,2,512]{2,1,0:T(2,128)(2,1)} %stack.14), calls=%async_computation.2 | async-start | bytes 1048576 | tf_op jit(solution)/shard_map/all_to_all | solution.py:146
  646.7 630.1 %all-gather = bf16[256,2,512]{2,1,0:T(2,128)(2,1)S(1)} all-gather(bf16[1,2,512]{2,1,0:T(2,128)(2,1)S(1)} %bitcast.393), channel_id=1, replica_groups=mesh['sess'=32,'dp'=4,'fsdp'=2] {'sess','dp','fsdp'}, dimensions={0}, use_global_device_ids=true | all-gather | bytes 526336 | tf_op jit(solution)/shard_map/all_gather | solution.py:144
  (217 shorter events, 35.5 us)
Async XLA Ops:
  7.2 70.8 %copy-start = (bf16[512,512]{1,0:T(8,128)(2,1)S(1)}, bf16[512,512]{1,0:T(8,128)(2,1)}, u32[]{:S(2)}) copy-start(bf16[512,512]{1,0:T(8,128)(2,1)} %param.23) | copy-start | bytes 1572868
  11.1 54.3 %all-to-all-start = ((bf16[32,2,2]{1,2,0:T(2,128)(2,1)}), bf16[32,2,2]{1,2,0:T(2,128)(2,1)S(1)}, u32[]{:S(2)}, u32[]{:S(2)}) async-start(bf16[32,2,2]{1,2,0:T(2,128)(2,1)} %copy.217), calls=%async_computation | async-start | bytes 32768 | tf_op jit(solution)/shard_map/all_to_all | solution.py:71
  65.4 12.3 copy-start.24
  65.4 12.5 copy-start.25
  65.4 12.5 copy-start.26
  65.4 380.7 %all-to-all-start.1 = ((bf16[32,2,131072]{2,1,0:T(2,128)(2,1)}), bf16[32,2,131072]{2,1,0:T(2,128)(2,1)}, u32[]{:S(2)}, u32[]{:S(2)}) async-start(bf16[32,2,131072]{2,1,0:T(2,128)(2,1)} %copy.220), calls=%async_computation.1 | async-start | bytes 33554432 | tf_op jit(solution)/shard_map/all_to_all | solution.py:70
  75.5 399.7 %all-gather.5.cloned.1.call-start = ((), (), s32[]{:S(2)}) async-start(), calls=%async_computation.3 | async-start | bytes 1572864 | tf_op jit(solution)/shard_map/all_gather | solution.py:17
  76.3 550.9 %all-gather.7.cloned.1.call-start = ((), (), s32[]{:S(2)}) async-start(), calls=%async_computation.4 | async-start | bytes 3145728 | tf_op jit(solution)/shard_map/all_gather | solution.py:21
  77.0 552.9 %all-gather.9.cloned.1.call-start = ((), (), s32[]{:S(2)}) async-start(), calls=%async_computation.5 | async-start | bytes 1572864 | tf_op jit(solution)/shard_map/all_gather | solution.py:25
  555.7 5.4 copy-start.15
  555.7 6.1 copy-start.2
  555.9 7.7 copy-start.14
  561.1 4.8 copy-start.13
  563.5 4.7 copy-start.12
  565.9 4.7 copy-start.11
  568.3 4.8 copy-start.10
  570.7 4.8 copy-start.9
  573.0 4.8 copy-start.8
  575.5 4.7 copy-start.7
  577.8 5.0 copy-start.6
  580.2 5.0 copy-start.5
  582.8 4.7 copy-start.4
  585.1 4.7 copy-start.3
  594.6 8.4 copy-start.16
  598.4 17.4 %copy-start.17 = (f32[32,64,64]{2,0,1:T(8,128)S(1)}, f32[32,64,64]{2,0,1:T(8,128)}, u32[]{:S(2)}) copy-start(f32[32,64,64]{2,0,1:T(8,128)} %convolution_bitcast_fusion.8) | copy-start | bytes 1572868
  600.7 16.1 %copy-start.18 = (f32[32,64,64]{2,0,1:T(8,128)S(1)}, f32[32,64,64]{2,0,1:T(8,128)}, u32[]{:S(2)}) copy-start(f32[32,64,64]{2,0,1:T(8,128)} %convolution_bitcast_fusion.9) | copy-start | bytes 1572868
  603.0 14.8 %copy-start.19 = (f32[32,64,64]{2,0,1:T(8,128)S(1)}, f32[32,64,64]{2,0,1:T(8,128)}, u32[]{:S(2)}) copy-start(f32[32,64,64]{2,0,1:T(8,128)} %convolution_bitcast_fusion.10) | copy-start | bytes 1572868
  604.1 14.8 %copy-start.20 = (f32[32,64,64]{2,0,1:T(8,128)S(1)}, f32[32,64,64]{2,0,1:T(8,128)}, u32[]{:S(2)}) copy-start(f32[32,64,64]{2,0,1:T(8,128)} %convolution_bitcast_fusion.11) | copy-start | bytes 1572868
  606.4 13.6 %copy-start.21 = (f32[32,64,64]{2,0,1:T(8,128)S(1)}, f32[32,64,64]{2,0,1:T(8,128)}, u32[]{:S(2)}) copy-start(f32[32,64,64]{2,0,1:T(8,128)} %convolution_bitcast_fusion.12) | copy-start | bytes 1572868
  608.9 12.1 copy-start.22
  611.2 10.9 copy-start.23
  626.4 652.5 %copy-start.1 = (bf16[512,512]{1,0:T(8,128)(2,1)S(1)}, bf16[512,512]{1,0:T(8,128)(2,1)}, u32[]{:S(2)}) copy-start(bf16[512,512]{1,0:T(8,128)(2,1)} %param.23) | copy-start | bytes 1572868
  632.8 644.8 %all-to-all-start.2 = ((bf16[256,2,512]{2,1,0:T(2,128)(2,1)}), bf16[256,2,512]{2,1,0:T(2,128)(2,1)S(1)}, u32[]{:S(2)}, u32[]{:S(2)}) async-start(bf16[256,2,512]{2,1,0:T(2,128)(2,1)} %stack.14), calls=%async_computation.2 | async-start | bytes 1048576 | tf_op jit(solution)/shard_map/all_to_all | solution.py:146
Sparse Core Ops, SparseCore 0:
  78.1 54.6 all-gather.4
  134.6 56.9 all-gather.6
  193.4 53.8 all-gather.8
